TPU v7x, 32 devices: a whole 2x2x4 slice. The times are simulated.
32 devices in a mesh: xy: 16 (over z, y, core), gz: 2 (over x).
Axes of the slice: x: 2, y: 2, z: 4, core: 2. Of those that a mesh axis runs over, the one named last changes fastest.
Arguments:
- hidden_features: bfloat16 [16, 16, 16, 512], P('gz', None, 'xy'), may hold values from -6 to 6
- scaling_factors_prenormal: float32 [512], replicated, may hold values from 0.1 to 1.9
- attention_input_matrices: bfloat16 [3, 512, 1536], P(None, 'xy'), may hold values from -1 to 1
- final_projection_matrices: bfloat16 [3, 512, 512], P(None, 'xy'), may hold values from -0.25 to 0.25
- score_scaling: float32 [3, 8], replicated, may hold values from 0 to 40
- filled_pillar_positions: int32 [16, 16], P('xy'), may hold values from 0 to 15, as said below
- filled_pillar_totals: int32 [16], P('xy'), may hold values from 4 to 16, as said below
Outputs:
- block_out: bfloat16 [16, 16, 16, 512], P('gz', None, 'xy')
Inputs may be any that keep to these rules, and one draw needn't show every extreme that they name: Row t of filled_pillar_positions is a permutation of 0 to 15; an entry c names the column x = c, y = t. `filled_pillar_totals`: some tile has all of its 16 columns occupied.
All inputs are finite; a program needn't handle non-finite values.
Results may differ from a plain program's by a relative error of at most 0.012.
Values may be sent and summed in bfloat16 or wider, within the bound.
No kernel may reach another device: no remote copies, remote signals or barrier semaphores. Data moves between devices by JAX's collectives and lax.ppermute only.
A program may use at most 64 MiB of HBM per device.

v0:
```python
import math
import jax
import jax.numpy as jnp
from jax import lax
from jax.sharding import PartitionSpec as P

EPSILON = 1e-06


def rms_scale(vector_rows):
    return vector_rows * lax.rsqrt(
        jnp.mean(vector_rows * vector_rows, axis=-1, keepdims=True) + EPSILON
    )


def project_qkv(tokens_in, w_project, attention_parts_number):
    projected = jnp.dot(tokens_in, w_project, preferred_element_type=jnp.float32)
    outer_shape = projected.shape[:-1]
    channels = w_project.shape[0]
    split_rows = projected.reshape(
        outer_shape + (3, attention_parts_number, channels // attention_parts_number)
    )
    queries = (
        rms_scale(split_rows[..., 0, :, :]).reshape(outer_shape + (channels,)).astype(jnp.bfloat16)
    )
    key_rows = (
        rms_scale(split_rows[..., 1, :, :]).reshape(outer_shape + (channels,)).astype(jnp.bfloat16)
    )
    values = split_rows[..., 2, :, :].reshape(outer_shape + (channels,)).astype(jnp.bfloat16)
    return (queries, key_rows, values)


def softmax_over_fibers(queries, key_rows, values, temper_row):
    attention_parts_number = temper_row.shape[0]
    outer_size, query_len, inner_size, channels = queries.shape
    key_len = key_rows.shape[1]
    head_dim = channels // attention_parts_number
    query_heads = queries.reshape(
        outer_size, query_len, inner_size, attention_parts_number, head_dim
    )
    key_heads = key_rows.reshape(outer_size, key_len, inner_size, attention_parts_number, head_dim)
    value_heads = values.reshape(outer_size, key_len, inner_size, attention_parts_number, head_dim)
    scores = jnp.einsum(
        "anbhd,ambhd->abhnm", query_heads, key_heads, preferred_element_type=jnp.float32
    )
    scores = scores * (temper_row / math.sqrt(head_dim))[None, None, :, None, None]
    weights = jax.nn.softmax(scores, axis=-1).astype(jnp.bfloat16)
    mixture = jnp.einsum(
        "abhnm,ambhd->anbhd", weights, value_heads, preferred_element_type=jnp.float32
    )
    return mixture.astype(jnp.bfloat16).reshape(outer_size, query_len, inner_size, channels)


def out_project(mixture, w_back):
    return jnp.dot(mixture, w_back, preferred_element_type=jnp.float32).astype(jnp.bfloat16)


def shards(
    hidden_features,
    scaling_factors_prenormal,
    attention_input_matrices,
    final_projection_matrices,
    score_scaling,
    filled_pillar_positions,
    filled_pillar_totals,
):
    full_qkv, full_out = (
        lax.all_gather(attention_input_matrices, "xy", axis=1, tiled=True),
        lax.all_gather(final_projection_matrices, "xy", axis=1, tiled=True),
    )
    attention_parts_number = score_scaling.shape[1]
    x_local, z_cells, y_rows, channels = hidden_features.shape
    normed = (rms_scale(hidden_features.astype(jnp.float32)) * scaling_factors_prenormal).astype(
        jnp.bfloat16
    )
    y_lines = normed.reshape(x_local * z_cells, y_rows, channels)
    local_query, local_keys, local_values = project_qkv(
        y_lines, full_qkv[1], attention_parts_number
    )
    query_along_y, keys_along_y, values_along_y = (
        lax.all_to_all(local_query, "xy", split_axis=0, concat_axis=1, tiled=True),
        lax.all_to_all(local_keys, "xy", split_axis=0, concat_axis=1, tiled=True),
        lax.all_to_all(local_values, "xy", split_axis=0, concat_axis=1, tiled=True),
    )
    y_mix = softmax_over_fibers(
        query_along_y[:, :, None, :],
        keys_along_y[:, :, None, :],
        values_along_y[:, :, None, :],
        score_scaling[1],
    )[:, :, 0, :]
    second_direction_answer = lax.all_to_all(
        out_project(y_mix, full_out[1]), "xy", split_axis=1, concat_axis=0, tiled=True
    ).reshape(hidden_features.shape)
    pieces = project_qkv(
        lax.all_to_all(normed, "gz", split_axis=1, concat_axis=0, tiled=True),
        full_qkv[0],
        attention_parts_number,
    )
    full_len, slab_part, items, _ = pieces[0].shape
    shaped = (1, full_len, slab_part * items, channels)
    x_mix = softmax_over_fibers(
        pieces[0].reshape(shaped),
        pieces[1].reshape(shaped),
        pieces[2].reshape(shaped),
        score_scaling[0],
    )
    result_rows = out_project(x_mix, full_out[0]).reshape(full_len, slab_part, items, channels)
    first_direction_answer = lax.all_to_all(
        result_rows, "gz", split_axis=0, concat_axis=1, tiled=True
    )
    cols_here = x_local * y_rows
    total_cols = filled_pillar_positions.shape[1]
    my_cols = lax.axis_index("gz") * cols_here + jnp.arange(cols_here, dtype=jnp.int32)
    live_rank = jnp.arange(total_cols, dtype=jnp.int32) < filled_pillar_totals[0]
    matches = filled_pillar_positions[0][None, :] == my_cols[:, None]
    live = jnp.any(jnp.logical_and(matches, live_rank[None, :]), axis=1)
    vertical_asking_terms, vertical_matching_terms, vertical_content_terms = project_qkv(
        normed, full_qkv[2], attention_parts_number
    )
    vertical_blended = softmax_over_fibers(
        vertical_asking_terms, vertical_matching_terms, vertical_content_terms, score_scaling[2]
    )
    z_full = out_project(vertical_blended, full_out[2])
    live_grid = live.reshape(x_local, 1, y_rows, 1)
    vertical_answer = jnp.where(live_grid, z_full, jnp.zeros_like(z_full))
    summed = (
        hidden_features.astype(jnp.float32)
        + first_direction_answer.astype(jnp.float32)
        + second_direction_answer.astype(jnp.float32)
    )
    summed = summed + vertical_answer.astype(jnp.float32)
    return summed.astype(jnp.bfloat16)


def solution(mesh):
    in_specs = (
        P("gz", None, "xy", None),
        P(),
        P(None, "xy", None),
        P(None, "xy", None),
        P(),
        P("xy", None),
        P("xy"),
    )
    out_specs = P("gz", None, "xy", None)
    return jax.shard_map(shards, mesh=mesh, in_specs=in_specs, out_specs=out_specs, check_vma=False)
```

profile of v0, /device:TPU:0, one launch (start us, length us, event | category | flops | bytes accessed | tf_op | source)
XLA Modules:
  0.0 148.3 jit_solution(13666185661406171766)
XLA Ops:
  6.5 0.7 all-gather.3.cloned.1.call-update
  7.3 1.0 fusion.23
  8.3 1.0 fusion.25
  9.3 0.7 copy.102
  10.0 4.2 %all-to-all-start = ((bf16[8,16,1,512]{3,0,2,1:T(8,128)(2,1)}), bf16[8,16,1,512]{3,0,2,1:T(8,128)(2,1)S(1)}, u32[]{:S(2)}, u32[]{:S(2)}) async-start(bf16[8,16,1,512]{3,0,2,1:T(8,128)(2,1)} %copy.102), calls=%async_computation | async-start | bytes 262144 | tf_op jit(solution)/shard_map/all_to_all | solution.py:95
  14.3 0.7 all-gather.5.cloned.1.call-update
  15.0 0.8 multiply_bitcast_fusion.2
  16.5 0.8 and_reduce_fusion
  17.3 1.5 %all-to-all-done = bf16[8,16,1,512]{3,0,2,1:T(8,128)(2,1)S(1)} async-done(((bf16[8,16,1,512]{3,0,2,1:T(8,128)(2,1)}), bf16[8,16,1,512]{3,0,2,1:T(8,128)(2,1)S(1)}, u32[]{:S(2)}, u32[]{:S(2)}) %all-to-all-start) | async-done | bytes 131104 | tf_op jit(solution)/shard_map/all_to_all | solution.py:95
  18.8 0.7 copy.103
  19.5 46.0 %all-gather.3.cloned.1.call-done = bf16[3,512,1536]{2,1,0:T(8,128)(2,1)} async-done(((bf16[3,32,1536]{2,1,0:T(8,128)(2,1)}), bf16[3,512,1536]{2,1,0:T(8,128)(2,1)}) %all-gather.3.cloned.1.call-update) | async-done | bytes 4718608 | tf_op jit(solution)/shard_map/all_gather | solution.py:68
  65.5 4.4 %slice_bitcast_fusion.2 = (bf16[1536,512]{0,1:T(8,128)(2,1)}, bf16[1536,512]{0,1:T(8,128)(2,1)S(1)}, bf16[1536,512]{0,1:T(8,128)(2,1)}) fusion(bf16[3,512,1536]{2,1,0:T(8,128)(2,1)} %all-gather.3.cloned.1.call-done), kind=kLoop, calls=%fused_computation.5 | loop fusion | bytes 9437184 | tf_op jit(solution)/shard_map/dot_general | solution.py:17
  69.9 1.7 %copy.104 = bf16[1536,512]{1,0:T(8,128)(2,1)S(1)} copy(bf16[1536,512]{0,1:T(8,128)(2,1)} %get-tuple-element.11) | data formatting | bytes 3145728 | tf_op jit(solution)/shard_map/dot_general | solution.py:17
  71.6 2.6 %copy.112 = bf16[1536,512]{1,0:T(8,128)(2,1)} copy(bf16[1536,512]{0,1:T(8,128)(2,1)} %get-tuple-element.13) | data formatting | bytes 3145728 | tf_op jit(solution)/shard_map/dot_general | solution.py:17
  74.3 2.0 %convolution_bitcast_fusion.2 = f32[128,1,3,8,64]{0,4,3,2,1:T(8,128)S(1)} fusion(bf16[128,512,1,1]{1,0,3,2:T(8,128)(2,1)S(1)} %bitcast.200, bf16[3,8,64,512]{3,2,1,0:T(8,128)(2,1)} %bitcast.199), kind=kOutput, calls=%fused_computation.8 | convolution fusion | flops 201326592 | bytes 2490368 | tf_op jit(solution)/shard_map/dot_general | solution.py:17
  76.3 0.9 copy-done
  77.3 0.5 broadcast.203
  77.8 1.2 reduce.26
  79.0 1.0 copy.180
  80.1 0.7 reshape.552
  80.8 3.5 %all-to-all-start.3 = ((bf16[16,2,2048]{2,1,0:T(2,128)(2,1)}), bf16[16,2,2048]{2,1,0:T(2,128)(2,1)S(1)}, u32[]{:S(2)}, u32[]{:S(2)}) async-start(bf16[16,2,2048]{2,1,0:T(2,128)(2,1)} %reshape.552), calls=%async_computation.3 | async-start | bytes 262144 | tf_op jit(solution)/shard_map/all_to_all | solution.py:81
  84.3 1.8 %convolution_bitcast_fusion.1 = f32[16,8,1,3,8,64]{5,1,4,3,0,2:T(8,128)S(1)} fusion(bf16[16,8,512,1,1]{2,1,4,3,0:T(8,128)(2,1)} %bitcast.207, bf16[3,8,64,512,1]{3,2,1,0,4:T(8,128)(2,1)S(1)} %bitcast.197), kind=kOutput, calls=%fused_computation.7 | convolution fusion | flops 201326592 | bytes 2490368 | tf_op jit(solution)/shard_map/dot_general | solution.py:17
  86.1 0.4 multiply_reduce_fusion.3
  86.5 0.4 fusion.22
  86.9 0.8 fusion.60
  87.7 1.0 fusion.9
  88.7 0.6 reduce.25
  89.3 0.1 copy.179
  89.4 0.7 reshape.550
  90.1 0.7 copy.125
  90.8 0.9 convolution_bitcast_fusion
  91.8 0.4 all-to-all-done.3
  92.2 5.8 %all-to-all-start.4 = ((bf16[16,2,2048]{2,1,0:T(2,128)(2,1)}), bf16[16,2,2048]{2,1,0:T(2,128)(2,1)S(1)}, u32[]{:S(2)}, u32[]{:S(2)}) async-start(bf16[16,2,2048]{2,1,0:T(2,128)(2,1)} %reshape.550), calls=%async_computation.4 | async-start | bytes 262144 | tf_op jit(solution)/shard_map/all_to_all | solution.py:82
  97.9 0.3 multiply_reduce_fusion.1
  98.3 1.0 slice.122
  99.3 0.2 reshape.524
  99.6 0.6 reduce.27
  100.1 0.1 copy.181
  100.3 0.7 reshape.554
  101.0 5.2 %all-to-all-done.4 = bf16[16,2,2048]{2,1,0:T(2,128)(2,1)S(1)} async-done(((bf16[16,2,2048]{2,1,0:T(2,128)(2,1)}), bf16[16,2,2048]{2,1,0:T(2,128)(2,1)S(1)}, u32[]{:S(2)}, u32[]{:S(2)}) %all-to-all-start.4) | async-done | bytes 131104 | tf_op jit(solution)/shard_map/all_to_all | solution.py:82
  106.2 3.5 %all-to-all-start.2 = ((bf16[16,2,2048]{2,1,0:T(2,128)(2,1)}), bf16[16,2,2048]{2,1,0:T(2,128)(2,1)S(1)}, u32[]{:S(2)}, u32[]{:S(2)}) async-start(bf16[16,2,2048]{2,1,0:T(2,128)(2,1)} %reshape.554), calls=%async_computation.2 | async-start | bytes 262144 | tf_op jit(solution)/shard_map/all_to_all | solution.py:83
  109.8 2.0 %fusion.54 = (f32[8,8,16]{2,1,0:T(8,128)}, f32[8,8,16,16]{2,3,1,0:T(8,128)}) fusion(f32[8,16,1,3,8,64]{5,1,4,3,0,2:T(8,128)S(1)} %convolution_bitcast_fusion, f32[8]{0:T(128)S(1)} %get-tuple-element.19, f32[8,16,8]{1,2,0:T(8,128)S(1)} %get-tuple-element.27, f32[8,16,8]{1,2,0:T(8,128)S(1)} %get-tuple-element.28), kind=kOutput, calls=%fused_computation.99 | convolution fusion | flops 2408463 | bytes 1184256 | tf_op jit(solution)/shard_map/sub | solution.py:47
  111.7 0.1 reshape.553
  111.9 0.2 reshape.548
  112.1 0.1 reshape.551
  112.2 0.2 reshape.549
  112.4 5.2 %all-to-all-done.2 = bf16[16,2,2048]{2,1,0:T(2,128)(2,1)S(1)} async-done(((bf16[16,2,2048]{2,1,0:T(2,128)(2,1)}), bf16[16,2,2048]{2,1,0:T(2,128)(2,1)S(1)}, u32[]{:S(2)}, u32[]{:S(2)}) %all-to-all-start.2) | async-done | bytes 131104 | tf_op jit(solution)/shard_map/all_to_all | solution.py:83
  117.6 0.1 reshape.555
  117.8 0.2 reshape.547
  118.0 0.5 fusion.55
  118.5 0.3 fusion.10
  118.8 0.1 copy.123
  118.9 0.2 squeeze_reshape.3
  119.1 1.3 convolution_convert_fusion.4
  120.4 0.7 copy.124
  121.2 3.6 %all-to-all-start.5 = ((bf16[8,16,512]{2,0,1:T(8,128)(2,1)}), bf16[8,16,512]{2,0,1:T(8,128)(2,1)S(1)}, u32[]{:S(2)}, u32[]{:S(2)}) async-start(bf16[8,16,512]{2,0,1:T(8,128)(2,1)} %copy.124), calls=%async_computation.5 | async-start | bytes 262144 | tf_op jit(solution)/shard_map/all_to_all | solution.py:91
  124.8 1.3 fusion.11
  126.1 0.1 copy.127
  126.2 0.2 reshape.533
  126.4 0.9 fusion.12
  127.3 5.3 %all-to-all-done.5 = bf16[8,16,512]{2,0,1:T(8,128)(2,1)S(1)} async-done(((bf16[8,16,512]{2,0,1:T(8,128)(2,1)}), bf16[8,16,512]{2,0,1:T(8,128)(2,1)S(1)}, u32[]{:S(2)}, u32[]{:S(2)}) %all-to-all-start.5) | async-done | bytes 131104 | tf_op jit(solution)/shard_map/all_to_all | solution.py:91
  132.7 3.4 %all-to-all-start.1 = ((bf16[16,8,1,512]{3,1,2,0:T(8,128)(2,1)}), bf16[16,8,1,512]{3,1,2,0:T(8,128)(2,1)S(1)}, u32[]{:S(2)}, u32[]{:S(2)}) async-start(bf16[16,8,1,512]{3,1,2,0:T(8,128)(2,1)} %fusion.12), calls=%async_computation.1 | async-start | bytes 262144 | tf_op jit(solution)/shard_map/all_to_all | solution.py:108
  136.1 4.4 %all-to-all-done.1 = bf16[16,8,1,512]{3,1,2,0:T(8,128)(2,1)S(1)} async-done(((bf16[16,8,1,512]{3,1,2,0:T(8,128)(2,1)}), bf16[16,8,1,512]{3,1,2,0:T(8,128)(2,1)S(1)}, u32[]{:S(2)}, u32[]{:S(2)}) %all-to-all-start.1) | async-done | bytes 131104 | tf_op jit(solution)/shard_map/all_to_all | solution.py:108
  140.5 0.9 fusion.18
  (29 shorter events, 0.5 us)
Async XLA Ops:
  6.5 59.0 %all-gather.3.cloned.1.call-start = ((), (), s32[]{:S(2)}) async-start(), calls=%async_computation.6 | async-start | bytes 5013504 | tf_op jit(solution)/shard_map/all_gather | solution.py:68
  10.0 8.8 %all-to-all-start = ((bf16[8,16,1,512]{3,0,2,1:T(8,128)(2,1)}), bf16[8,16,1,512]{3,0,2,1:T(8,128)(2,1)S(1)}, u32[]{:S(2)}, u32[]{:S(2)}) async-start(bf16[8,16,1,512]{3,0,2,1:T(8,128)(2,1)} %copy.102), calls=%async_computation | async-start | bytes 262144 | tf_op jit(solution)/shard_map/all_to_all | solution.py:95
  14.3 104.9 %all-gather.5.cloned.1.call-start = ((), (), s32[]{:S(2)}) async-start(), calls=%async_computation.7 | async-start | bytes 1671168 | tf_op jit(solution)/shard_map/all_gather | solution.py:69
  76.2 0.9 copy-start
  80.8 11.4 %all-to-all-start.3 = ((bf16[16,2,2048]{2,1,0:T(2,128)(2,1)}), bf16[16,2,2048]{2,1,0:T(2,128)(2,1)S(1)}, u32[]{:S(2)}, u32[]{:S(2)}) async-start(bf16[16,2,2048]{2,1,0:T(2,128)(2,1)} %reshape.552), calls=%async_computation.3 | async-start | bytes 262144 | tf_op jit(solution)/shard_map/all_to_all | solution.py:81
  91.7 7.5 %copy-start.3 = (bf16[1,16,8,8,64]{4,1,3,2,0:T(8,128)(2,1)S(1)}, bf16[1,16,8,8,64]{4,1,3,2,0:T(8,128)(2,1)}, u32[]{:S(2)}) copy-start(bf16[1,16,8,8,64]{4,1,3,2,0:T(8,128)(2,1)} %fusion.9) | copy-start | bytes 393220
  92.2 14.1 %all-to-all-start.4 = ((bf16[16,2,2048]{2,1,0:T(2,128)(2,1)}), bf16[16,2,2048]{2,1,0:T(2,128)(2,1)S(1)}, u32[]{:S(2)}, u32[]{:S(2)}) async-start(bf16[16,2,2048]{2,1,0:T(2,128)(2,1)} %reshape.550), calls=%async_computation.4 | async-start | bytes 262144 | tf_op jit(solution)/shard_map/all_to_all | solution.py:82
  106.2 11.4 %all-to-all-start.2 = ((bf16[16,2,2048]{2,1,0:T(2,128)(2,1)}), bf16[16,2,2048]{2,1,0:T(2,128)(2,1)S(1)}, u32[]{:S(2)}, u32[]{:S(2)}) async-start(bf16[16,2,2048]{2,1,0:T(2,128)(2,1)} %reshape.554), calls=%async_computation.2 | async-start | bytes 262144 | tf_op jit(solution)/shard_map/all_to_all | solution.py:83
  118.8 6.0 %copy-start.4 = (f32[8,8,16]{2,1,0:T(8,128)S(1)}, f32[8,8,16]{2,1,0:T(8,128)}, u32[]{:S(2)}) copy-start(f32[8,8,16]{2,1,0:T(8,128)} %get-tuple-element.21) | copy-start | bytes 12292
  121.1 5.3 %copy-start.2 = (bf16[3,512,512]{2,1,0:T(8,128)(2,1)S(1)}, bf16[3,512,512]{2,1,0:T(8,128)(2,1)}, u32[]{:S(2)}) copy-start(bf16[3,512,512]{2,1,0:T(8,128)(2,1)} %all-gather.5.cloned.1.call-done) | copy-start | bytes 4718596
  121.2 11.5 %all-to-all-start.5 = ((bf16[8,16,512]{2,0,1:T(8,128)(2,1)}), bf16[8,16,512]{2,0,1:T(8,128)(2,1)S(1)}, u32[]{:S(2)}, u32[]{:S(2)}) async-start(bf16[8,16,512]{2,0,1:T(8,128)(2,1)} %copy.124), calls=%async_computation.5 | async-start | bytes 262144 | tf_op jit(solution)/shard_map/all_to_all | solution.py:91
  126.1 14.4 %copy-start.1 = (bf16[8,16,1,512]{3,1,2,0:T(8,128)(2,1)S(1)}, bf16[8,16,1,512]{3,1,2,0:T(8,128)(2,1)}, u32[]{:S(2)}) copy-start(bf16[8,16,1,512]{3,1,2,0:T(8,128)(2,1)} %param.7) | copy-start | bytes 393220
  132.7 7.8 %all-to-all-start.1 = ((bf16[16,8,1,512]{3,1,2,0:T(8,128)(2,1)}), bf16[16,8,1,512]{3,1,2,0:T(8,128)(2,1)S(1)}, u32[]{:S(2)}, u32[]{:S(2)}) async-start(bf16[16,8,1,512]{3,1,2,0:T(8,128)(2,1)} %fusion.12), calls=%async_computation.1 | async-start | bytes 262144 | tf_op jit(solution)/shard_map/all_to_all | solution.py:108
Sparse Core Ops, SparseCore 0:
  9.6 55.8 all-gather.2
  67.7 39.1 all-gather.4
where the time goes:
time: 149 us; the launch traced here: 148 us
  waiting for transfers between devices  69.6 us (47%)
  starting transfers between devices  24.1 us (16%)
  local copies, waits for them, and re-layouts  19.2 us (13%)
  between operations  14.4 us (10%)
  matrix products  13.7 us (9%)
  other arithmetic  7.31 us (5%)
    all_gather x1, waiting for transfers between devices, shards(): lax.all_gather(attention_input_matrices, 'xy', axis=1, tiled=True)  46 us
    dot_general x4, local copies, waits for them, and re-layouts, project_qkv(): jnp.dot(tokens_in, w_project, preferred_element_type=jnp.float32)  9.41 us
    all_to_all x1, starting transfers between devices, shards(): lax.all_to_all(local_keys, 'xy', split_axis=0, concat_axis=1, tiled=True)  5.78 us
    all_to_all x1, waiting for transfers between devices, shards(): lax.all_to_all(out_project(y_mix, full_out[1]), 'xy', split_axis=1, conca...  5.35 us
    all_to_all x1, waiting for transfers between devices, shards(): lax.all_to_all(local_keys, 'xy', split_axis=0, concat_axis=1, tiled=True)  5.24 us
    all_to_all x1, waiting for transfers between devices, shards(): lax.all_to_all(local_values, 'xy', split_axis=0, concat_axis=1, tiled=True)  5.21 us
    dot_general x3, matrix products, project_qkv(): jnp.dot(tokens_in, w_project, preferred_element_type=jnp.float32)  4.68 us
    unnamed x22, local copies, waits for them, and re-layouts  4.68 us
  transfers between devices with their start and end apart: 8, of which 7 were waited for; matrix products, arithmetic and copies ran while one was open for 25% of the time, Pallas kernels for 0%

commit v1 on v0

--- a/solution.py
+++ b/solution.py
@@ -5,6 +5,13 @@
 from jax.sharding import PartitionSpec as P
 
 EPSILON = 1e-06
+
+
+def stacked_exchange(value, mesh_axis, split, join):
+    devices = lax.axis_size(mesh_axis)
+    tiles = jnp.stack(jnp.split(value, devices, axis=split), axis=0)
+    tiles = lax.all_to_all(tiles, mesh_axis, split_axis=0, concat_axis=0)
+    return jnp.concatenate(tiles, axis=join)
 
 
 def rms_scale(vector_rows):
@@ -79,7 +86,7 @@
     )
     query_along_y, keys_along_y, values_along_y = (
         lax.all_to_all(local_query, "xy", split_axis=0, concat_axis=1, tiled=True),
-        lax.all_to_all(local_keys, "xy", split_axis=0, concat_axis=1, tiled=True),
+        stacked_exchange(local_keys, "xy", 0, 1),
         lax.all_to_all(local_values, "xy", split_axis=0, concat_axis=1, tiled=True),
     )
     y_mix = softmax_over_fibers(

time: 149 us -> 191 us (1.28)
  local copies, waits for them, and re-layouts: 19.2 us -> 60.6 us
    another operation x5 -> x21, local copies, waits for them, and re-layouts: 0.97 us -> 24.8 us  [the longest x16 22.9 us: stacked_exchange(): tiles = jnp.stack(jnp.split(value, devices, axis=split), axis=0)]
    unnamed x22 -> x39, local copies, waits for them, and re-layouts: 4.68 us -> 20.7 us
    all_to_all x1, waiting for transfers between devices: 5.24 us -> 0.01 us  [stacked_exchange(): tiles = lax.all_to_all(tiles, mesh_axis, split_axis=0, concat_axis=0)]
    all_to_all x1, waiting for transfers between devices: 0.39 us -> 4.77 us  [shards(): lax.all_to_all(local_query, 'xy', split_axis=0, concat_axis=1, tiled=True)]
    split x0 -> x2, local copies, waits for them, and re-layouts: none -> 2.81 us  [stacked_exchange(): tiles = jnp.stack(jnp.split(value, devices, axis=split), axis=0)]
    all_to_all x1, starting transfers between devices: 3.51 us -> 6.05 us  [shards(): lax.all_to_all(local_query, 'xy', split_axis=0, concat_axis=1, tiled=True)]
  transfers between devices with their start and end apart: 8 -> 8, of which waited for: 7 -> 6; matrix products, arithmetic and copies ran while one was open for 25% -> 41% of each run, Pallas kernels for 0% -> 0%
where the time goes in v1:
time: 191 us; the launch traced here: 189 us
  waiting for transfers between devices  68.1 us (36%)
  local copies, waits for them, and re-layouts  60.6 us (32%)
  starting transfers between devices  25 us (13%)
  between operations  14.5 us (8%)
  matrix products  13.6 us (7%)
  other arithmetic  7.36 us (4%)
    all_gather x1, waiting for transfers between devices, shards(): lax.all_gather(attention_input_matrices, 'xy', axis=1, tiled=True)  46.7 us
    another operation x16, local copies, waits for them, and re-layouts, stacked_exchange(): tiles = jnp.stack(jnp.split(value, devices, axis=split), axis=0)  22.9 us
    unnamed x39, local copies, waits for them, and re-layouts  20.7 us
    dot_general x4, local copies, waits for them, and re-layouts, project_qkv(): jnp.dot(tokens_in, w_project, preferred_element_type=jnp.float32)  8.8 us
    all_to_all x1, starting transfers between devices, shards(): lax.all_to_all(local_query, 'xy', split_axis=0, concat_axis=1, tiled=True)  6.05 us
    all_to_all x1, waiting for transfers between devices, shards(): lax.all_to_all(out_project(y_mix, full_out[1]), 'xy', split_axis=1, conca...  5.35 us
    dot_general x3, matrix products, project_qkv(): jnp.dot(tokens_in, w_project, preferred_element_type=jnp.float32)  5.2 us
    all_to_all x1, waiting for transfers between devices, shards(): lax.all_to_all(local_values, 'xy', split_axis=0, concat_axis=1, tiled=True)  5.04 us
  transfers between devices with their start and end apart: 8, of which 6 were waited for; matrix products, arithmetic and copies ran while one was open for 41% of the time, Pallas kernels for 0%

profile of v1, /device:TPU:0, one launch (start us, length us, event | category | flops | bytes accessed | tf_op | source)
XLA Modules:
  0.0 189.1 jit_solution(14396144874076290056)
XLA Ops:
  7.3 1.0 fusion.23
  8.3 1.0 fusion.25
  9.3 0.7 copy.132
  10.0 4.2 %all-to-all-start = ((bf16[8,16,1,512]{3,0,2,1:T(8,128)(2,1)}), bf16[8,16,1,512]{3,0,2,1:T(8,128)(2,1)S(1)}, u32[]{:S(2)}, u32[]{:S(2)}) async-start(bf16[8,16,1,512]{3,0,2,1:T(8,128)(2,1)} %copy.132), calls=%async_computation | async-start | bytes 262144 | tf_op jit(solution)/shard_map/all_to_all | solution.py:102
  14.3 0.7 all-gather.5.cloned.1.call-update
  15.0 1.4 multiply_bitcast_fusion.2
  17.0 1.4 and_reduce_fusion
  18.9 46.7 %all-gather.3.cloned.1.call-done = bf16[3,512,1536]{2,1,0:T(8,128)(2,1)} async-done(((bf16[3,32,1536]{2,1,0:T(8,128)(2,1)}), bf16[3,512,1536]{2,1,0:T(8,128)(2,1)}) %all-gather.3.cloned.1.call-update) | async-done | bytes 4718608 | tf_op jit(solution)/shard_map/all_gather | solution.py:75
  65.5 3.9 %slice_bitcast_fusion.2 = (bf16[1536,512]{0,1:T(8,128)(2,1)S(1)}, bf16[1536,512]{0,1:T(8,128)(2,1)S(1)}, bf16[1536,512]{0,1:T(8,128)(2,1)}) fusion(bf16[3,512,1536]{2,1,0:T(8,128)(2,1)} %all-gather.3.cloned.1.call-done), kind=kLoop, calls=%fused_computation.5 | loop fusion | bytes 9437184 | tf_op jit(solution)/shard_map/dot_general | solution.py:24
  69.4 2.6 %copy.142 = bf16[1536,512]{1,0:T(8,128)(2,1)} copy(bf16[1536,512]{0,1:T(8,128)(2,1)} %get-tuple-element.13) | data formatting | bytes 3145728 | tf_op jit(solution)/shard_map/dot_general | solution.py:24
  72.0 2.0 %convolution_bitcast_fusion.2 = f32[128,1,3,8,64]{0,4,3,2,1:T(8,128)S(1)} fusion(bf16[128,512,1,1]{1,0,3,2:T(8,128)(2,1)S(1)} %bitcast.228, bf16[3,8,64,512]{3,2,1,0:T(8,128)(2,1)} %bitcast.227), kind=kOutput, calls=%fused_computation.8 | convolution fusion | flops 201326592 | bytes 2490368 | tf_op jit(solution)/shard_map/dot_general | solution.py:24
  74.2 0.7 copy-done
  74.9 1.8 fusion.54
  76.8 1.0 copy.148
  78.3 1.6 copy.149
  79.9 1.6 copy.150
  81.5 1.6 copy.151
  83.1 1.6 copy.152
  84.6 1.6 copy.153
  86.2 1.6 copy.154
  87.8 1.6 copy.155
  89.3 1.6 copy.156
  90.9 1.6 copy.157
  92.5 1.6 copy.158
  94.0 1.6 copy.159
  95.6 1.6 copy.160
  97.2 1.6 copy.161
  98.7 1.0 copy.162
  99.7 1.0 copy.147
  100.7 1.3 constant_dynamic-update-slice_fusion.14
  102.0 1.3 constant_dynamic-update-slice_fusion.13
  103.3 1.3 constant_dynamic-update-slice_fusion.12
  104.6 1.3 constant_dynamic-update-slice_fusion.11
  105.9 1.3 constant_dynamic-update-slice_fusion.10
  107.1 1.3 constant_dynamic-update-slice_fusion.9
  108.4 1.3 constant_dynamic-update-slice_fusion.8
  109.7 1.3 constant_dynamic-update-slice_fusion.7
  111.0 1.3 constant_dynamic-update-slice_fusion.6
  112.3 1.3 constant_dynamic-update-slice_fusion.5
  113.6 1.3 constant_dynamic-update-slice_fusion.4
  114.9 1.3 constant_dynamic-update-slice_fusion.3
  116.2 1.3 constant_dynamic-update-slice_fusion.2
  118.7 4.2 %all-to-all-start.4 = ((bf16[16,8,1,512]{3,1,2,0:T(8,128)(2,1)}), bf16[16,8,1,512]{3,1,2,0:T(8,128)(2,1)}, u32[]{:S(2)}, u32[]{:S(2)}) async-start(bf16[16,8,1,512]{3,1,2,0:T(8,128)(2,1)} %constant_dynamic-update-slice_fusion), calls=%async_computation.4 | async-start | bytes 262144 | tf_op jit(solution)/shard_map/all_to_all | solution.py:13
  122.8 1.6 copy.134
  124.4 2.3 %convolution_bitcast_fusion.1 = f32[16,8,1,3,8,64]{5,1,4,3,0,2:T(8,128)S(1)} fusion(bf16[16,8,512,1,1]{2,1,4,3,0:T(8,128)(2,1)S(1)} %bitcast.234, bf16[3,8,64,512,1]{3,2,1,0,4:T(8,128)(2,1)} %bitcast.225), kind=kOutput, calls=%fused_computation.7 | convolution fusion | flops 201326592 | bytes 2490368 | tf_op jit(solution)/shard_map/dot_general | solution.py:24
  127.6 0.8 fusion.61
  128.3 1.0 fusion.9
  132.1 0.9 convolution_bitcast_fusion
  133.1 6.0 %all-to-all-start.3 = ((bf16[16,2,2048]{2,1,0:T(2,128)(2,1)}), bf16[16,2,2048]{2,1,0:T(2,128)(2,1)S(1)}, u32[]{:S(2)}, u32[]{:S(2)}) async-start(bf16[16,2,2048]{2,1,0:T(2,128)(2,1)} %reshape.553), calls=%async_computation.3 | async-start | bytes 262144 | tf_op jit(solution)/shard_map/all_to_all | solution.py:88
  139.5 1.0 slice.122
  142.3 4.8 %all-to-all-done.3 = bf16[16,2,2048]{2,1,0:T(2,128)(2,1)S(1)} async-done(((bf16[16,2,2048]{2,1,0:T(2,128)(2,1)}), bf16[16,2,2048]{2,1,0:T(2,128)(2,1)S(1)}, u32[]{:S(2)}, u32[]{:S(2)}) %all-to-all-start.3) | async-done | bytes 131104 | tf_op jit(solution)/shard_map/all_to_all | solution.py:88
  147.1 3.5 %all-to-all-start.2 = ((bf16[16,2,2048]{2,1,0:T(2,128)(2,1)}), bf16[16,2,2048]{2,1,0:T(2,128)(2,1)S(1)}, u32[]{:S(2)}, u32[]{:S(2)}) async-start(bf16[16,2,2048]{2,1,0:T(2,128)(2,1)} %reshape.555), calls=%async_computation.2 | async-start | bytes 262144 | tf_op jit(solution)/shard_map/all_to_all | solution.py:90
  150.6 1.4 fusion.55
  152.0 1.1 reshape.552
  153.4 5.0 %all-to-all-done.2 = bf16[16,2,2048]{2,1,0:T(2,128)(2,1)S(1)} async-done(((bf16[16,2,2048]{2,1,0:T(2,128)(2,1)}), bf16[16,2,2048]{2,1,0:T(2,128)(2,1)S(1)}, u32[]{:S(2)}, u32[]{:S(2)}) %all-to-all-start.2) | async-done | bytes 131104 | tf_op jit(solution)/shard_map/all_to_all | solution.py:90
  160.0 1.3 convolution_convert_fusion.4
  161.2 0.7 copy.169
  162.0 3.6 %all-to-all-start.5 = ((bf16[8,16,512]{2,0,1:T(8,128)(2,1)}), bf16[8,16,512]{2,0,1:T(8,128)(2,1)S(1)}, u32[]{:S(2)}, u32[]{:S(2)}) async-start(bf16[8,16,512]{2,0,1:T(8,128)(2,1)} %copy.169), calls=%async_computation.5 | async-start | bytes 262144 | tf_op jit(solution)/shard_map/all_to_all | solution.py:98
  165.6 1.3 fusion.11
  167.3 0.9 fusion.12
  168.2 5.3 %all-to-all-done.5 = bf16[8,16,512]{2,0,1:T(8,128)(2,1)S(1)} async-done(((bf16[8,16,512]{2,0,1:T(8,128)(2,1)}), bf16[8,16,512]{2,0,1:T(8,128)(2,1)S(1)}, u32[]{:S(2)}, u32[]{:S(2)}) %all-to-all-start.5) | async-done | bytes 131104 | tf_op jit(solution)/shard_map/all_to_all | solution.py:98
  173.5 3.4 %all-to-all-start.1 = ((bf16[16,8,1,512]{3,1,2,0:T(8,128)(2,1)}), bf16[16,8,1,512]{3,1,2,0:T(8,128)(2,1)S(1)}, u32[]{:S(2)}, u32[]{:S(2)}) async-start(bf16[16,8,1,512]{3,1,2,0:T(8,128)(2,1)} %fusion.12), calls=%async_computation.1 | async-start | bytes 262144 | tf_op jit(solution)/shard_map/all_to_all | solution.py:115
  176.9 4.4 %all-to-all-done.1 = bf16[16,8,1,512]{3,1,2,0:T(8,128)(2,1)S(1)} async-done(((bf16[16,8,1,512]{3,1,2,0:T(8,128)(2,1)}), bf16[16,8,1,512]{3,1,2,0:T(8,128)(2,1)S(1)}, u32[]{:S(2)}, u32[]{:S(2)}) %all-to-all-start.1) | async-done | bytes 131104 | tf_op jit(solution)/shard_map/all_to_all | solution.py:115
  181.3 0.9 fusion.18
  (63 shorter events, 10.9 us)
Async XLA Ops:
  6.5 59.0 %all-gather.3.cloned.1.call-start = ((), (), s32[]{:S(2)}) async-start(), calls=%async_computation.6 | async-start | bytes 5013504 | tf_op jit(solution)/shard_map/all_gather | solution.py:75
  10.0 8.8 %all-to-all-start = ((bf16[8,16,1,512]{3,0,2,1:T(8,128)(2,1)}), bf16[8,16,1,512]{3,0,2,1:T(8,128)(2,1)S(1)}, u32[]{:S(2)}, u32[]{:S(2)}) async-start(bf16[8,16,1,512]{3,0,2,1:T(8,128)(2,1)} %copy.132), calls=%async_computation | async-start | bytes 262144 | tf_op jit(solution)/shard_map/all_to_all | solution.py:102
  14.3 145.7 %all-gather.5.cloned.1.call-start = ((), (), s32[]{:S(2)}) async-start(), calls=%async_computation.7 | async-start | bytes 1671168 | tf_op jit(solution)/shard_map/all_gather | solution.py:76
  74.0 0.9 copy-start
  118.7 14.4 %all-to-all-start.4 = ((bf16[16,8,1,512]{3,1,2,0:T(8,128)(2,1)}), bf16[16,8,1,512]{3,1,2,0:T(8,128)(2,1)}, u32[]{:S(2)}, u32[]{:S(2)}) async-start(bf16[16,8,1,512]{3,1,2,0:T(8,128)(2,1)} %constant_dynamic-update-slice_fusion), calls=%async_computation.4 | async-start | bytes 262144 | tf_op jit(solution)/shard_map/all_to_all | solution.py:13
  126.7 0.8 copy-start.7
  133.1 8.9 %copy-start.3 = (bf16[1,16,8,8,64]{4,1,3,2,0:T(8,128)(2,1)S(1)}, bf16[1,16,8,8,64]{4,1,3,2,0:T(8,128)(2,1)}, u32[]{:S(2)}) copy-start(bf16[1,16,8,8,64]{4,1,3,2,0:T(8,128)(2,1)} %fusion.9) | copy-start | bytes 393220
  133.1 14.0 %all-to-all-start.3 = ((bf16[16,2,2048]{2,1,0:T(2,128)(2,1)}), bf16[16,2,2048]{2,1,0:T(2,128)(2,1)S(1)}, u32[]{:S(2)}, u32[]{:S(2)}) async-start(bf16[16,2,2048]{2,1,0:T(2,128)(2,1)} %reshape.553), calls=%async_computation.3 | async-start | bytes 262144 | tf_op jit(solution)/shard_map/all_to_all | solution.py:88
  139.2 11.4 %copy-start.6 = (f32[8]{0:T(128)S(1)}, f32[8]{0:T(128)}, u32[]{:S(2)}) copy-start(f32[8]{0:T(128)} %get-tuple-element.35) | copy-start | bytes 100
  147.1 11.4 %all-to-all-start.2 = ((bf16[16,2,2048]{2,1,0:T(2,128)(2,1)}), bf16[16,2,2048]{2,1,0:T(2,128)(2,1)S(1)}, u32[]{:S(2)}, u32[]{:S(2)}) async-start(bf16[16,2,2048]{2,1,0:T(2,128)(2,1)} %reshape.555), calls=%async_computation.2 | async-start | bytes 262144 | tf_op jit(solution)/shard_map/all_to_all | solution.py:90
  152.0 6.8 %copy-start.5 = (f32[8]{0:T(128)S(1)}, f32[8]{0:T(128)}, u32[]{:S(2)}) copy-start(f32[8]{0:T(128)} %get-tuple-element.36) | copy-start | bytes 100
  162.0 5.3 %copy-start.2 = (bf16[3,512,512]{2,1,0:T(8,128)(2,1)S(1)}, bf16[3,512,512]{2,1,0:T(8,128)(2,1)}, u32[]{:S(2)}) copy-start(bf16[3,512,512]{2,1,0:T(8,128)(2,1)} %all-gather.5.cloned.1.call-done) | copy-start | bytes 4718596
  162.0 11.5 %all-to-all-start.5 = ((bf16[8,16,512]{2,0,1:T(8,128)(2,1)}), bf16[8,16,512]{2,0,1:T(8,128)(2,1)S(1)}, u32[]{:S(2)}, u32[]{:S(2)}) async-start(bf16[8,16,512]{2,0,1:T(8,128)(2,1)} %copy.169), calls=%async_computation.5 | async-start | bytes 262144 | tf_op jit(solution)/shard_map/all_to_all | solution.py:98
  167.0 14.4 %copy-start.1 = (bf16[8,16,1,512]{3,1,2,0:T(8,128)(2,1)S(1)}, bf16[8,16,1,512]{3,1,2,0:T(8,128)(2,1)}, u32[]{:S(2)}) copy-start(bf16[8,16,1,512]{3,1,2,0:T(8,128)(2,1)} %param.7) | copy-start | bytes 393220
  167.0 14.4 %copy-start.4 = (pred[8]{0:T(512)(128)(4,1)S(1)}, pred[8]{0:T(512)(128)(4,1)}, u32[]{:S(2)}) copy-start(pred[8]{0:T(512)(128)(4,1)} %and_reduce_fusion) | copy-start | bytes 28
  173.5 7.8 %all-to-all-start.1 = ((bf16[16,8,1,512]{3,1,2,0:T(8,128)(2,1)}), bf16[16,8,1,512]{3,1,2,0:T(8,128)(2,1)S(1)}, u32[]{:S(2)}, u32[]{:S(2)}) async-start(bf16[16,8,1,512]{3,1,2,0:T(8,128)(2,1)} %fusion.12), calls=%async_computation.1 | async-start | bytes 262144 | tf_op jit(solution)/shard_map/all_to_all | solution.py:115
Sparse Core Ops, SparseCore 0:
  9.6 55.8 all-gather.2
  67.7 38.1 all-gather.4
